TPU v7x, 32 devices: a whole 2x2x4 slice. The times are simulated.
32 devices in a mesh: wide: 16 (over z, y, x), narrow: 2 (over core).
Axes of the slice: x: 2, y: 2, z: 4, core: 2. Of those that a mesh axis runs over, the one named last changes fastest.
Arguments:
- grads: bfloat16 [14, 512, 2048], P(None, 'wide', 'narrow'), may hold values from -200 to 200
- momentum: float32 [14, 512, 2048], P(None, 'wide', 'narrow'), may hold values from -400 to 400
- owners: int32 [14], replicated, may hold values from 0 to 15, as said below
- norm_grads: float32 [28, 2048], P('narrow', 'wide'), may hold values from -6 to 6
- norm_params: float32 [28, 2048], P('narrow', 'wide'), may hold values from 0.5 to 1.5
- adam_m: float32 [28, 2048], P('narrow', 'wide'), may hold values from -4 to 4
- adam_v: float32 [28, 2048], P('narrow', 'wide'), may hold values from 0.1 to 4
Outputs:
- muon_update: bfloat16 [14, 512, 2048], P(None, 'wide', 'narrow')
- momentum_new: float32 [14, 512, 2048], P(None, 'wide', 'narrow')
- owner_load: float32 [16], P('wide')
- norm_params_new: float32 [28, 2048], P('narrow', 'wide')
- adam_m_new: float32 [28, 2048], P('narrow', 'wide')
- adam_v_new: float32 [28, 2048], P('narrow', 'wide')
Inputs may be any that keep to these rules, and one draw needn't show every extreme that they name: `owners`: each of the 16 groups owns at most 2 matrices, and some group owns exactly 2.
All inputs are finite; a program needn't handle non-finite values.
Results may differ from a plain program's by a relative error of at most 0.014.
Values may be sent and summed in bfloat16 or wider, within the bound.
A program may use at most 64 MiB of HBM per device.

v0:
```python
import math
import jax
import jax.numpy as jnp
from jax import lax
from jax.sharding import PartitionSpec as P

D = 2048
KV_OUT = 512
ITERS = 2
coef_a = 3.4445
coef_b = -4.775
coef_c = 2.0315
muon_beta = 0.95
norm_eps = 1e-07
adam_first = 0.9
adam_second = 0.95
adam_rate = 0.02
adam_eps = 1e-08
first_fix = 1.0 - 0.9**10
second_fix = 1.0 - 0.95**10


def polynomial_times(current, partial_value):
    gram_sum = lax.psum(partial_value.astype(jnp.bfloat16), "narrow")
    square = jnp.einsum("cmk,ckn->cmn", gram_sum, gram_sum, preferred_element_type=jnp.float32)
    polynomial = (coef_b * gram_sum.astype(jnp.float32) + coef_c * square).astype(jnp.bfloat16)
    return jnp.einsum("cmk,ckn->cmn", polynomial, current, preferred_element_type=jnp.float32)


def newton_schulz(current):
    result = current.astype(jnp.float32)
    for iteration in range(ITERS):
        partial_value = jnp.einsum(
            "cmk,cnk->cmn", current, current, preferred_element_type=jnp.float32
        )
        product_bx = polynomial_times(current, partial_value)
        result = coef_a * current.astype(jnp.float32) + product_bx
        if iteration + 1 < ITERS:
            current = result.astype(jnp.bfloat16)
    updates = (math.sqrt(D) * result).astype(jnp.bfloat16)
    update_values = updates.astype(jnp.float32)
    update_squares = lax.psum(jnp.sum(update_values * update_values, axis=(1, 2)), "narrow")
    return (updates[None], (update_squares / (KV_OUT * D))[None])


def orthogonalize(slot_block):
    directions = slot_block[0]
    square_sums = lax.psum(jnp.sum(directions * directions, axis=(1, 2)), "narrow")
    current = (directions / (jnp.sqrt(square_sums)[:, None, None] + norm_eps)).astype(jnp.bfloat16)
    return newton_schulz(current)


def on_device(grads, momentum, owners, norm_grads, norm_params, adam_m, adam_v):
    grad_values = grads.astype(jnp.float32)
    momentum_new = muon_beta * momentum + grad_values
    direction = grad_values + muon_beta * momentum_new
    groups = lax.axis_size("wide")
    matrix_count = owners.shape[0]
    matrix_ids = jnp.arange(matrix_count, dtype=jnp.int32)
    capacity = -(-matrix_count // groups)
    slot_of = matrix_ids % groups * capacity + matrix_ids // groups
    slot_total = groups * capacity
    slot_match = slot_of[None, :] == jnp.arange(slot_total, dtype=jnp.int32)[:, None]
    source = jnp.sum(jnp.where(slot_match, matrix_ids[None, :], 0), axis=1) + jnp.where(
        jnp.any(slot_match, axis=1), 0, matrix_count
    )
    row_count = direction.shape[1]
    col_count = direction.shape[2]
    padded = jnp.concatenate([direction, jnp.zeros((1, row_count, col_count), jnp.float32)], axis=0)
    outgoing = jnp.take(padded, source, axis=0).reshape(groups, capacity, row_count, col_count)
    updates, slot_loads = orthogonalize(
        lax.all_to_all(outgoing, "wide", split_axis=0, concat_axis=2, tiled=True)
    )
    returned = lax.all_to_all(updates, "wide", split_axis=2, concat_axis=0, tiled=True)
    arrived = returned.reshape(slot_total, row_count, col_count)
    muon_update = jnp.take(arrived, slot_of, axis=0)
    own_group = lax.axis_index("wide")
    computed_here = matrix_ids % groups == own_group
    local_loads = jnp.where(computed_here, jnp.take(slot_loads[0], matrix_ids // groups), 0.0)
    matrix_loads = lax.psum(local_loads, "wide")
    owner_load = jnp.sum(jnp.where(owners == own_group, matrix_loads, 0.0)).reshape(1)
    adam_m_new = adam_first * adam_m + (1.0 - adam_first) * norm_grads
    adam_v_new = adam_second * adam_v + (1.0 - adam_second) * norm_grads * norm_grads
    corrected = adam_m_new / first_fix / (jnp.sqrt(adam_v_new / second_fix) + adam_eps)
    norm_params_new = norm_params - adam_rate * corrected
    return (muon_update, momentum_new, owner_load, norm_params_new, adam_m_new, adam_v_new)


def solution(mesh):
    return jax.shard_map(
        on_device,
        mesh=mesh,
        in_specs=(
            P(None, "wide", "narrow"),
            P(None, "wide", "narrow"),
            P(),
            P("narrow", "wide"),
            P("narrow", "wide"),
            P("narrow", "wide"),
            P("narrow", "wide"),
        ),
        out_specs=(
            P(None, "wide", "narrow"),
            P(None, "wide", "narrow"),
            P("wide"),
            P("narrow", "wide"),
            P("narrow", "wide"),
            P("narrow", "wide"),
        ),
        check_vma=False,
    )
```

profile of v0, /device:TPU:0, one launch (start us, length us, event | category | flops | bytes accessed | tf_op | source)
XLA Modules:
  0.0 207.1 jit_solution(12475647661025235217)
XLA Ops:
  7.2 0.0 all-reduce.4.cloned.1.call-start
  7.2 0.1 fusion.20
  7.3 0.1 select_reduce_fusion
  7.5 3.5 %convert_add_fusion = (f32[14,32,1024]{2,1,0:T(8,128)S(1)}, f32[14,32,1024]{2,1,0:T(8,128)}) fusion(bf16[14,32,1024]{2,1,0:T(8,128)(2,1)} %param.7, f32[14,32,1024]{2,1,0:T(8,128)} %param.8), kind=kLoop, calls=%fused_computation.2 | loop fusion | flops 2293760 | bytes 6422528 | tf_op jit(solution)/shard_map/add | solution.py:56
  11.0 0.3 concatenate.3
  11.2 2.0 gather_fusion
  13.3 1.8 bitcast_select_fusion
  15.1 57.0 %all_to_all.8 = f32[16,1,32,1024]{3,2,1,0:T(8,128)S(1)} all-to-all(f32[16,1,32,1024]{3,2,1,0:T(8,128)S(1)} %bitcast_select_fusion), channel_id=1, replica_groups=mesh['wide'=16,'narrow'=2] {'wide'}, dimensions={0} | all-to-all | bytes 4194304 | tf_op jit(solution)/shard_map/all_to_all | solution.py:72
  72.1 1.1 multiply_reduce_fusion.1
  73.2 3.1 %psum.35 = f32[1]{0:T(128)} all-reduce(f32[1]{0:T(128)} %bitcast.3), channel_id=1, replica_groups=mesh['wide'=16,'narrow'=2] {'narrow'}, use_global_device_ids=true, to_apply=%region_3.4 | all-reduce | flops 1 | bytes 8 | tf_op jit(solution)/shard_map/psum | solution.py:48
  77.0 1.7 convert_multiply_fusion
  78.7 1.5 fusion.7
  80.2 0.0 all-reduce.4.cloned.1.call-update
  80.3 0.2 all-reduce.6.cloned.1.call-start
  80.5 16.9 %all-reduce.4.cloned.1.call-done = bf16[1,512,512]{2,1,0:T(8,128)(2,1)} async-done(((bf16[1,512,512]{2,1,0:T(8,128)(2,1)}), bf16[1,512,512]{2,1,0:T(8,128)(2,1)}) %all-reduce.4.cloned.1.call-update) | async-done | bytes 524304 | tf_op jit(solution)/shard_map/psum | solution.py:24
  97.4 3.4 %fusion = bf16[512,1024]{1,0:T(8,128)(2,1)} fusion(f32[16,1,32,1024]{3,2,1,0:T(8,128)S(1)} %copy-done, bf16[512,1024]{1,0:T(8,128)(2,1)S(1)} %bitcast.81, bf16[1,512,512]{2,1,0:T(8,128)(2,1)} %all-reduce.4.cloned.1.call-done), kind=kOutput, calls=%fused_computation.5 | convolution fusion | flops 807665664 | bytes 4718592 | tf_op jit(solution)/shard_map/cmk,ckn->cmn/dot_general | solution.py:27
  100.8 3.2 %fusion.8 = bf16[1,512,512]{2,1,0:T(8,128)(2,1)} fusion(bf16[512,1024]{1,0:T(8,128)(2,1)} %fusion), kind=kOutput, calls=%fused_computation.23 | convolution fusion | flops 537133056 | bytes 1572864 | tf_op jit(solution)/shard_map/cmk,cnk->cmn/dot_general | solution.py:33
  104.0 20.1 %all-reduce.6.cloned.1.call-done = bf16[1,512,512]{2,1,0:T(8,128)(2,1)} async-done(((bf16[1,512,512]{2,1,0:T(8,128)(2,1)}), bf16[1,512,512]{2,1,0:T(8,128)(2,1)}) %all-reduce.6.cloned.1.call-update) | async-done | bytes 524304 | tf_op jit(solution)/shard_map/psum | solution.py:24
  124.1 3.2 %multiply_reduce_fusion = (f32[]{:T(128)}, bf16[512,1024]{1,0:T(8,128)(2,1)S(1)}) fusion(bf16[512,1024]{1,0:T(8,128)(2,1)S(1)} %copy-done.6, bf16[1,512,512]{2,1,0:T(8,128)(2,1)} %all-reduce.6.cloned.1.call-done), kind=kOutput, calls=%fused_computation.7 | convolution fusion | flops 810811392 | bytes 2621444 | tf_op jit(solution)/shard_map/cmk,ckn->cmn/dot_general | solution.py:27
  127.3 1.6 copy.18
  128.9 0.5 broadcast.355
  129.5 6.8 %reduce.3 = bf16[512,1024]{1,0:T(8,128)(2,1)S(1)} reduce(bf16[512,1,1,1024]{3,2,1,0:T(2,128)(2,1)S(1)} %bitcast.77, bf16[]{:T(256)} %broadcast.355), dimensions={1,2}, to_apply=%bitcast.75.reduce_sub_computation | reduce | bytes 2097154
  136.3 1.6 reshape.253
  137.9 6.8 %all-to-all-start.1 = ((bf16[16,2,16384]{2,1,0:T(2,128)(2,1)}), bf16[16,2,16384]{2,1,0:T(2,128)(2,1)S(1)}, u32[]{:S(2)}, u32[]{:S(2)}) async-start(bf16[16,2,16384]{2,1,0:T(2,128)(2,1)} %reshape.253), calls=%async_computation.1 | async-start | bytes 2097152 | tf_op jit(solution)/shard_map/all_to_all | solution.py:74
  144.8 0.6 multiply_subtract_fusion
  145.4 3.1 %psum.38 = f32[1]{0:T(128)} all-reduce(f32[1]{0:T(128)} %bitcast.17), channel_id=1, replica_groups=mesh['wide'=16,'narrow'=2] {'narrow'}, use_global_device_ids=true, to_apply=%region_7.8 | all-reduce | flops 1 | bytes 8 | tf_op jit(solution)/shard_map/psum | solution.py:42
  149.2 47.4 %psum.39 = f32[14]{0:T(128)S(1)} all-reduce(f32[14]{0:T(128)S(1)} %compare_select_fusion.5), channel_id=1, replica_groups=mesh['wide'=16,'narrow'=2] {'wide'}, use_global_device_ids=true, to_apply=%region_8.9 | all-reduce | flops 14 | bytes 112 | tf_op jit(solution)/shard_map/psum | solution.py:80
  196.6 0.6 fusion.23
  197.2 1.0 reshape.254
  198.2 0.4 copy.16
  198.6 0.6 gather_fusion.1
  199.2 1.1 broadcast_select_fusion
  (24 shorter events, 0.1 us)
Async XLA Ops:
  7.2 90.2 %all-reduce.4.cloned.1.call-start = ((), (), s32[]{:S(2)}) async-start(), calls=%async_computation.2 | async-start | bytes 1048576 | tf_op jit(solution)/shard_map/psum | solution.py:24
  78.7 18.7 %copy-start = (f32[16,1,32,1024]{3,2,1,0:T(8,128)S(1)}, f32[16,1,32,1024]{3,2,1,0:T(8,128)}, u32[]{:S(2)}) copy-start(f32[16,1,32,1024]{3,2,1,0:T(8,128)} %get-tuple-element.9) | copy-start | bytes 6291460
  80.3 43.8 %all-reduce.6.cloned.1.call-start = ((), (), s32[]{:S(2)}) async-start(), calls=%async_computation.3 | async-start | bytes 1048576 | tf_op jit(solution)/shard_map/psum | solution.py:24
  100.8 23.3 %copy-start.6 = (bf16[512,1024]{1,0:T(8,128)(2,1)S(1)}, bf16[512,1024]{1,0:T(8,128)(2,1)}, u32[]{:S(2)}) copy-start(bf16[512,1024]{1,0:T(8,128)(2,1)} %fusion) | copy-start | bytes 3145732
  136.2 8.5 %copy-start.1 = (f32[14,128]{1,0:T(8,128)S(1)}, f32[14,128]{1,0:T(8,128)}, u32[]{:S(2)}) copy-start(f32[14,128]{1,0:T(8,128)} %param.11) | copy-start | bytes 21508
  136.3 8.5 %copy-start.2 = (f32[14,128]{1,0:T(8,128)S(1)}, f32[14,128]{1,0:T(8,128)}, u32[]{:S(2)}) copy-start(f32[14,128]{1,0:T(8,128)} %param.10) | copy-start | bytes 21508
  136.3 8.5 %copy-start.3 = (f32[14,128]{1,0:T(8,128)S(1)}, f32[14,128]{1,0:T(8,128)}, u32[]{:S(2)}) copy-start(f32[14,128]{1,0:T(8,128)} %param.12) | copy-start | bytes 21508
  136.3 8.5 %copy-start.4 = (f32[14,128]{1,0:T(8,128)S(1)}, f32[14,128]{1,0:T(8,128)}, u32[]{:S(2)}) copy-start(f32[14,128]{1,0:T(8,128)} %param.13) | copy-start | bytes 21508
  136.3 60.3 %copy-start.5 = (s32[14]{0:T(128)S(1)}, s32[14]{0:T(128)}, u32[]{:S(2)}) copy-start(s32[14]{0:T(128)} %param.9) | copy-start | bytes 172
  137.9 59.3 %all-to-all-start.1 = ((bf16[16,2,16384]{2,1,0:T(2,128)(2,1)}), bf16[16,2,16384]{2,1,0:T(2,128)(2,1)S(1)}, u32[]{:S(2)}, u32[]{:S(2)}) async-start(bf16[16,2,16384]{2,1,0:T(2,128)(2,1)} %reshape.253), calls=%async_computation.1 | async-start | bytes 2097152 | tf_op jit(solution)/shard_map/all_to_all | solution.py:74
Sparse Core Ops, SparseCore 0:
  80.4 16.9 all-reduce.3
  104.1 19.9 all-reduce.5
where the time goes:
time: 208 us; the launch traced here: 207 us
  blocking collectives  111 us (53%)
  waiting for transfers between devices  37 us (18%)
  other arithmetic  17.5 us (8%)
  between operations  15.6 us (8%)
  matrix products  11.3 us (5%)
  local copies, waits for them, and re-layouts  8.1 us (4%)
  starting transfers between devices  7.05 us (3%)
    all_to_all x1, blocking collectives, on_device(): lax.all_to_all(outgoing, 'wide', split_axis=0, concat_axis=2, tiled=True)  57 us
    psum x1, blocking collectives, on_device(): matrix_loads = lax.psum(local_loads, 'wide')  47.4 us
    psum x2, waiting for transfers between devices, polynomial_times(): gram_sum = lax.psum(partial_value.astype(jnp.bfloat16), 'narrow')  37 us
    all_to_all x1, starting transfers between devices, on_device(): lax.all_to_all(updates, 'wide', split_axis=2, concat_axis=0, tiled=True)  6.79 us
    unnamed x1, other arithmetic  6.78 us
    dot_general x2, matrix products, polynomial_times(): jnp.einsum('cmk,ckn->cmn', polynomial, current, preferred_element_type=jn...  6.64 us
    dot_general x2, matrix products, newton_schulz(): jnp.einsum('cmk,cnk->cmn', current, current, preferred_element_type=jnp.f...  4.71 us
  transfers between devices with their start and end apart: 3, of which 2 were waited for; matrix products, arithmetic and copies ran while one was open for 1% of the time, Pallas kernels for 0%

commit v1 on v0

--- a/solution.py
+++ b/solution.py
@@ -3,6 +3,7 @@
 import jax.numpy as jnp
 from jax import lax
 from jax.sharding import PartitionSpec as P
+from jax.lax import all_gather
 
 D = 2048
 KV_OUT = 512
@@ -21,7 +22,7 @@
 
 
 def polynomial_times(current, partial_value):
-    gram_sum = lax.psum(partial_value.astype(jnp.bfloat16), "narrow")
+    gram_sum = all_gather(partial_value.astype(jnp.bfloat16), axis_name="narrow").sum(axis=0)
     square = jnp.einsum("cmk,ckn->cmn", gram_sum, gram_sum, preferred_element_type=jnp.float32)
     polynomial = (coef_b * gram_sum.astype(jnp.float32) + coef_c * square).astype(jnp.bfloat16)
     return jnp.einsum("cmk,ckn->cmn", polynomial, current, preferred_element_type=jnp.float32)

time: 208 us -> 191 us (0.918)
  waiting for transfers between devices: 37 us -> 17.6 us
  other arithmetic: 17.5 us -> 21.5 us
    psum x2 -> x0, waiting for transfers between devices: 37 us -> none  [polynomial_times(): gram_sum = lax.psum(partial_value.astype(jnp.bfloat16), 'narrow')]
    all_gather x0 -> x2, waiting for transfers between devices: none -> 17.6 us  [polynomial_times(): all_gather(partial_value.astype(jnp.bfloat16), axis_name='narrow')]
    reduce_sum x0 -> x2, other arithmetic: none -> 4.01 us  [polynomial_times(): all_gather(partial_value.astype(jnp.bfloat16), axis_name='narrow')]
where the time goes in v1:
time: 191 us
  blocking collectives  111 us (58%)
  other arithmetic  21.5 us (11%)
  waiting for transfers between devices  17.6 us (9%)
  between operations  15.6 us (8%)
  matrix products  10.2 us (5%)
  local copies, waits for them, and re-layouts  8.1 us (4%)
  starting transfers between devices  7.03 us (4%)
    all_to_all x1, blocking collectives, on_device(): lax.all_to_all(outgoing, 'wide', split_axis=0, concat_axis=2, tiled=True)  57 us
    psum x1, blocking collectives, on_device(): matrix_loads = lax.psum(local_loads, 'wide')  47.4 us
    all_gather x2, waiting for transfers between devices, polynomial_times(): all_gather(partial_value.astype(jnp.bfloat16), axis_name='narrow')  17.6 us
    unnamed x1, other arithmetic  6.78 us
    all_to_all x1, starting transfers between devices, on_device(): lax.all_to_all(updates, 'wide', split_axis=2, concat_axis=0, tiled=True)  6.77 us
    dot_general x2, matrix products, polynomial_times(): jnp.einsum('cmk,ckn->cmn', polynomial, current, preferred_element_type=jn...  5.51 us
    dot_general x2, matrix products, newton_schulz(): jnp.einsum('cmk,cnk->cmn', current, current, preferred_element_type=jnp.f...  4.71 us
    reduce_sum x2, other arithmetic, polynomial_times(): all_gather(partial_value.astype(jnp.bfloat16), axis_name='narrow')  4.01 us
  transfers between devices with their start and end apart: 3, of which 2 were waited for; matrix products, arithmetic and copies ran while one was open for 1% of the time, Pallas kernels for 0%

profile of v1, /device:TPU:0, one launch (start us, length us, event | category | flops | bytes accessed | tf_op | source)
XLA Modules:
  0.0 190.6 jit_solution(5172679001927111768)
XLA Ops:
  7.2 0.1 fusion.14
  7.3 0.1 select_reduce_fusion
  7.5 3.5 %convert_add_fusion = (f32[14,32,1024]{2,1,0:T(8,128)S(1)}, f32[14,32,1024]{2,1,0:T(8,128)}) fusion(bf16[14,32,1024]{2,1,0:T(8,128)(2,1)} %param.7, f32[14,32,1024]{2,1,0:T(8,128)} %param.8), kind=kLoop, calls=%fused_computation.2 | loop fusion | flops 2293760 | bytes 6422528 | tf_op jit(solution)/shard_map/add | solution.py:57
  11.0 0.3 concatenate.3
  11.2 2.0 %gather_fusion = f32[16,32,1024]{2,1,0:T(8,128)} fusion(f32[15,32,1024]{2,1,0:T(8,128)S(1)} %concatenate.3, s32[1024]{0:T(1024)S(1)} %pad_clamp_fusion.1), kind=kCustom, calls=%fused_computation | custom fusion | bytes 4194368 | tf_op jit(solution)/shard_map/jit(_take)/gather | solution.py:71
  13.3 1.8 bitcast_select_fusion
  15.1 57.0 %all_to_all.8 = f32[16,1,32,1024]{3,2,1,0:T(8,128)S(1)} all-to-all(f32[16,1,32,1024]{3,2,1,0:T(8,128)S(1)} %bitcast_select_fusion), channel_id=1, replica_groups=mesh['wide'=16,'narrow'=2] {'wide'}, dimensions={0} | all-to-all | bytes 4194304 | tf_op jit(solution)/shard_map/all_to_all | solution.py:73
  72.1 1.1 multiply_reduce_fusion.1
  73.2 3.1 %psum.21 = f32[1]{0:T(128)} all-reduce(f32[1]{0:T(128)} %bitcast.3), channel_id=1, replica_groups=mesh['wide'=16,'narrow'=2] {'narrow'}, use_global_device_ids=true, to_apply=%region_3.4 | all-reduce | flops 1 | bytes 8 | tf_op jit(solution)/shard_map/psum | solution.py:49
  77.0 1.7 convert_multiply_fusion
  78.7 1.5 convolution_convert_fusion.1
  80.3 0.2 all-gather.7.cloned.1.call-start
  80.5 7.2 %all-gather.5.cloned.1.call-done = bf16[1024,512]{1,0:T(8,128)(2,1)} async-done(((bf16[512,512]{1,0:T(8,128)(2,1)}), bf16[1024,512]{1,0:T(8,128)(2,1)}) %all-gather.5.cloned.1.call-update) | async-done | bytes 1048592 | tf_op jit(solution)/shard_map/all_gather | solution.py:25
  87.7 2.3 %reduce.7 = bf16[512,512]{1,0:T(8,128)(2,1)} reduce(bf16[2,512,512]{2,1,0:T(8,128)(2,1)} %bitcast.40, bf16[]{:T(256)} %constant.119.clone.1), dimensions={0}, to_apply=%region_4.5 | reduce | flops 262144 | bytes 1572866 | tf_op jit(solution)/shard_map/reduce_sum | solution.py:25
  90.1 3.6 %fusion = bf16[512,1024]{1,0:T(8,128)(2,1)} fusion(f32[16,1,32,1024]{3,2,1,0:T(8,128)S(1)} %copy-done, bf16[512,1024]{1,0:T(8,128)(2,1)S(1)} %bitcast.43, bf16[512,512]{1,0:T(8,128)(2,1)} %reduce.7), kind=kOutput, calls=%fused_computation.5 | convolution fusion | flops 807665664 | bytes 4718592 | tf_op jit(solution)/shard_map/cmk,ckn->cmn/dot_general | solution.py:28
  93.7 3.2 %convolution_convert_fusion = bf16[512,512]{1,0:T(8,128)(2,1)} fusion(bf16[512,1024]{1,0:T(8,128)(2,1)} %fusion), kind=kOutput, calls=%fused_computation.18 | convolution fusion | flops 537133056 | bytes 1572864 | tf_op jit(solution)/shard_map/cmk,cnk->cmn/dot_general | solution.py:34
  96.9 10.4 %all-gather.7.cloned.1.call-done = bf16[1024,512]{1,0:T(8,128)(2,1)} async-done(((bf16[512,512]{1,0:T(8,128)(2,1)}), bf16[1024,512]{1,0:T(8,128)(2,1)}) %all-gather.7.cloned.1.call-update) | async-done | bytes 1048592 | tf_op jit(solution)/shard_map/all_gather | solution.py:25
  107.3 1.7 reduce.8
  108.9 1.9 multiply_reduce_fusion
  110.8 1.6 copy.18
  112.4 0.5 broadcast.357
  112.9 6.8 %reduce.9 = bf16[512,1024]{1,0:T(8,128)(2,1)S(1)} reduce(bf16[512,1,1,1024]{3,2,1,0:T(2,128)(2,1)S(1)} %bitcast.37, bf16[]{:T(256)} %broadcast.357), dimensions={1,2}, to_apply=%bitcast.35.reduce_sub_computation | reduce | bytes 2097154
  119.8 1.6 reshape.267
  121.4 6.8 %all-to-all-start.1 = ((bf16[16,2,16384]{2,1,0:T(2,128)(2,1)}), bf16[16,2,16384]{2,1,0:T(2,128)(2,1)S(1)}, u32[]{:S(2)}, u32[]{:S(2)}) async-start(bf16[16,2,16384]{2,1,0:T(2,128)(2,1)} %reshape.267), calls=%async_computation.1 | async-start | bytes 2097152 | tf_op jit(solution)/shard_map/all_to_all | solution.py:75
  128.3 0.6 multiply_subtract_fusion
  128.9 3.1 %psum.22 = f32[1]{0:T(128)} all-reduce(f32[1]{0:T(128)} %bitcast.11), channel_id=1, replica_groups=mesh['wide'=16,'narrow'=2] {'narrow'}, use_global_device_ids=true, to_apply=%region_7.8 | all-reduce | flops 1 | bytes 8 | tf_op jit(solution)/shard_map/psum | solution.py:43
  132.6 47.4 %psum.23 = f32[14]{0:T(128)S(1)} all-reduce(f32[14]{0:T(128)S(1)} %compare_select_fusion.5), channel_id=1, replica_groups=mesh['wide'=16,'narrow'=2] {'wide'}, use_global_device_ids=true, to_apply=%region_8.9 | all-reduce | flops 14 | bytes 112 | tf_op jit(solution)/shard_map/psum | solution.py:81
  180.1 0.6 fusion.17
  180.7 1.0 reshape.268
  181.7 0.4 copy.16
  182.1 0.6 gather_fusion.1
  182.7 1.1 broadcast_select_fusion
  (26 shorter events, 0.2 us)
Async XLA Ops:
  7.2 80.6 %all-gather.5.cloned.1.call-start = ((), (), s32[]{:S(2)}) async-start(), calls=%async_computation.2 | async-start | bytes 1572864 | tf_op jit(solution)/shard_map/all_gather | solution.py:25
  78.7 11.4 %copy-start = (f32[16,1,32,1024]{3,2,1,0:T(8,128)S(1)}, f32[16,1,32,1024]{3,2,1,0:T(8,128)}, u32[]{:S(2)}) copy-start(f32[16,1,32,1024]{3,2,1,0:T(8,128)} %get-tuple-element.9) | copy-start | bytes 6291460
  80.3 27.0 %all-gather.7.cloned.1.call-start = ((), (), s32[]{:S(2)}) async-start(), calls=%async_computation.3 | async-start | bytes 1572864 | tf_op jit(solution)/shard_map/all_gather | solution.py:25
  93.7 15.2 %copy-start.6 = (bf16[512,1024]{1,0:T(8,128)(2,1)S(1)}, bf16[512,1024]{1,0:T(8,128)(2,1)}, u32[]{:S(2)}) copy-start(bf16[512,1024]{1,0:T(8,128)(2,1)} %fusion) | copy-start | bytes 3145732
  119.7 8.5 %copy-start.1 = (f32[14,128]{1,0:T(8,128)S(1)}, f32[14,128]{1,0:T(8,128)}, u32[]{:S(2)}) copy-start(f32[14,128]{1,0:T(8,128)} %param.11) | copy-start | bytes 21508
  119.7 8.5 %copy-start.2 = (f32[14,128]{1,0:T(8,128)S(1)}, f32[14,128]{1,0:T(8,128)}, u32[]{:S(2)}) copy-start(f32[14,128]{1,0:T(8,128)} %param.10) | copy-start | bytes 21508
  119.8 8.5 %copy-start.3 = (f32[14,128]{1,0:T(8,128)S(1)}, f32[14,128]{1,0:T(8,128)}, u32[]{:S(2)}) copy-start(f32[14,128]{1,0:T(8,128)} %param.12) | copy-start | bytes 21508
  119.8 8.5 %copy-start.4 = (f32[14,128]{1,0:T(8,128)S(1)}, f32[14,128]{1,0:T(8,128)}, u32[]{:S(2)}) copy-start(f32[14,128]{1,0:T(8,128)} %param.13) | copy-start | bytes 21508
  119.8 60.3 %copy-start.5 = (s32[14]{0:T(128)S(1)}, s32[14]{0:T(128)}, u32[]{:S(2)}) copy-start(s32[14]{0:T(128)} %param.9) | copy-start | bytes 172
  121.4 59.3 %all-to-all-start.1 = ((bf16[16,2,16384]{2,1,0:T(2,128)(2,1)}), bf16[16,2,16384]{2,1,0:T(2,128)(2,1)S(1)}, u32[]{:S(2)}, u32[]{:S(2)}) async-start(bf16[16,2,16384]{2,1,0:T(2,128)(2,1)} %reshape.267), calls=%async_computation.1 | async-start | bytes 2097152 | tf_op jit(solution)/shard_map/all_to_all | solution.py:75
Sparse Core Ops, SparseCore 0:
  80.4 7.2 all-gather.4
  97.0 10.1 all-gather.6
